TPU v7x, 256 devices: a whole 4x4x8 slice. The times are simulated.
256 devices in a mesh: table: 32 (over z, x), scal: 8 (over y, core).
Axes of the slice: x: 4, y: 4, z: 8, core: 2. Of those that a mesh axis runs over, the one named last changes fastest.
Arguments:
- cell_coords: float32 [4, 524288], P(None, ('table', 'scal')), may hold values from 0 to 1
- flamelet_table: float32 [131072, 1024], P('table', 'scal'), may hold values from -15 to 15
- owner_shard: int32 [524288, 1], P(('table', 'scal')), may hold values from 0 to 31; in each aligned block of 64 rows (0 to 63, 64 to 127, ...) at most 5 rows name the same one
- local_bin: int32 [524288], P(('table', 'scal')), may hold values from 0 to 4095
Outputs:
- filtered_fields: float32 [32, 2048, 256], P(None, ('table', 'scal'))
- x_gradient: float32 [32, 2048, 256], P(None, ('table', 'scal'))
Inputs may be any that keep to these rules, and one draw needn't show every extreme that they name: `owner_shard`: in each aligned block of 64 rows (one group of one device's cells) no shard is named by more than 5 rows, a bound that some block reaches.
All inputs are finite; a program needn't handle non-finite values.
Results may differ from a plain program's by a relative error of at most 0.00012.
Values sent between devices are 32-bit elements; how exact they have to be, the bound alone decides.
A program may use at most 128 MiB of HBM per device.

v0:
```python
import jax
import jax.numpy as jnp
import numpy as np
from jax import lax
from jax.sharding import PartitionSpec as P

SCAL_ALL = 32
K = 32
BX = 8
LG = 8


strength = 0.499


def spline_weights(coords):
    linear = [jnp.stack([1.0 - coords[axis_id], coords[axis_id]]) for axis_id in range(3)]
    frac_last = coords[3]
    square = frac_last * frac_last
    cube = square * frac_last
    remain = 1.0 - frac_last
    cubic = jnp.stack(
        [
            remain * remain * remain / 6.0,
            (3.0 * cube - 6.0 * square + 4.0) / 6.0,
            (-3.0 * cube + 3.0 * square + 3.0 * frac_last + 1.0) / 6.0,
            cube / 6.0,
        ]
    )
    product = (
        linear[0][:, None, None, None, :]
        * linear[1][None, :, None, None, :]
        * linear[2][None, None, :, None, :]
        * cubic[None, None, None, :, :]
    )
    return product.reshape(-1, coords.shape[1])


def thomas_solve(below, middle, above, right_side):
    length = middle.shape[0]
    upper_factor = np.zeros(length)
    solved = np.zeros(right_side.shape)
    for row in range(length):
        if row == 0:
            denom = middle[0]
            solved[0] = right_side[0] / denom
        else:
            denom = middle[row] - below[row] * upper_factor[row - 1]
            solved[row] = (right_side[row] - below[row] * solved[row - 1]) / denom
        upper_factor[row] = above[row] / denom
    for row in range(length - 2, -1, -1):
        solved[row] = solved[row] - upper_factor[row] * solved[row + 1]
    return solved


def filter_table(length):
    positions = np.arange(length)
    offset = positions[None, :] - positions[:, None]
    distance = np.abs(offset)
    interior = (positions >= 3) & (positions <= length - 4)
    coeffs = [
        (11.0 + 10.0 * strength) / 16.0,
        (15.0 + 34.0 * strength) / 64.0,
        (-3.0 + 6.0 * strength) / 32.0,
        (1.0 - 2.0 * strength) / 64.0,
    ]
    band = np.zeros((length, length))
    for reach in range(4):
        band = band + np.where(distance == reach, coeffs[reach], 0.0)
    right_side = np.where(interior[:, None], band, np.where(offset == 0, 1.0, 0.0))
    coupling = np.where(interior, strength, 0.0)
    return thomas_solve(coupling, np.ones(length), coupling, right_side).astype(np.float32)


def derivative_table(length):
    positions = np.arange(length)
    offset = positions[None, :] - positions[:, None]
    distance = np.abs(offset)
    direction = np.sign(offset) * 1.0
    boundary = (positions == 0) | (positions == length - 1)
    second = (positions == 1) | (positions == length - 2)
    interior = ~(boundary | second)
    below_diag = np.where(
        interior, 1.0 / 3.0, np.where(second, 0.25, np.where(positions == length - 1, 2.0, 0.0))
    )
    above_diag = np.where(
        interior, 1.0 / 3.0, np.where(second, 0.25, np.where(positions == 0, 2.0, 0.0))
    )
    inner_rows = direction * (
        np.where(distance == 1, 7.0 / 9.0, 0.0) + np.where(distance == 2, 1.0 / 36.0, 0.0)
    )
    second_rows = direction * np.where(distance == 1, 0.75, 0.0)
    first_row = np.where(
        offset == 0, -2.5, np.where(offset == 1, 2.0, np.where(offset == 2, 0.5, 0.0))
    )
    final_row = np.where(
        offset == 0, 2.5, np.where(offset == -1, -2.0, np.where(offset == -2, -0.5, 0.0))
    )
    right_side = np.where(
        interior[:, None],
        inner_rows,
        np.where(
            second[:, None], second_rows, np.where((positions == 0)[:, None], first_row, final_row)
        ),
    )
    return thomas_solve(below_diag, np.ones(length), above_diag, right_side).astype(np.float32)


def on_device(cell_coords, flamelet_table, owner_shard, local_bin):
    table_count = lax.axis_size("table")
    scal_count = lax.axis_size("scal")
    cell_count = cell_coords.shape[1]
    group_size = cell_count // table_count
    capacity = max(2, 5 * group_size // (2 * table_count))
    slot_count = table_count * table_count * capacity
    group_slots = table_count * capacity
    owners = owner_shard[:, 0].reshape(table_count, group_size)
    matches = (
        owners[:, :, None] == jnp.arange(table_count, dtype=jnp.int32)[None, None, :]
    ).astype(jnp.int32)
    group_rank = jnp.sum((jnp.cumsum(matches, axis=1) - 1) * matches, axis=2)
    local_slot = owners * capacity + group_rank
    slot_ids = jnp.arange(group_slots, dtype=jnp.int32)
    placing = (local_slot[:, :, None] == slot_ids[None, None, :]).astype(jnp.float32)
    payload = jnp.concatenate(
        [local_bin.astype(jnp.float32)[None, :], cell_coords], axis=0
    ).reshape(5, table_count, group_size)
    placed = jnp.einsum("fgc,gcq->fgq", payload, placing, precision=lax.Precision.HIGHEST)
    outgoing = (
        placed.reshape(5, table_count, table_count, capacity)
        .transpose(0, 2, 1, 3)
        .reshape(5, table_count, group_slots)
    )
    received = lax.all_to_all(outgoing, "table", split_axis=1, concat_axis=1, tiled=True).reshape(
        5, slot_count
    )
    shard_piece = lax.all_gather(received, "scal", axis=1, tiled=True)
    weights = spline_weights(shard_piece[1:])
    table_rows = jnp.take(flamelet_table, shard_piece[0].astype(jnp.int32), axis=0)
    table_rows = table_rows.reshape(table_rows.shape[0], -1, K)
    looked = jnp.einsum("nsk,kn->sn", table_rows, weights, precision=lax.Precision.HIGHEST)
    looked = looked.reshape(looked.shape[0], scal_count, slot_count)
    grouped = lax.all_to_all(looked, "scal", split_axis=1, concat_axis=0, tiled=True).reshape(
        SCAL_ALL, table_count, table_count, capacity
    )
    length = BX * table_count
    replies = lax.all_to_all(grouped, "table", split_axis=1, concat_axis=1, tiled=True)
    by_group = replies.transpose(0, 2, 1, 3).reshape(SCAL_ALL, table_count, group_slots)
    values = jnp.einsum("sgq,gcq->sgc", by_group, placing, precision=lax.Precision.HIGHEST).reshape(
        SCAL_ALL, table_count, LG, BX
    )
    pencil = lax.all_to_all(values, "table", split_axis=1, concat_axis=3, tiled=True).reshape(
        SCAL_ALL * LG, length
    )
    filter_op = jnp.asarray(filter_table(length).T)
    derivative_op = jnp.asarray(derivative_table(length).T)
    filtered = jnp.dot(pencil, filter_op, precision=lax.Precision.HIGHEST)
    gradient = jnp.dot(filtered, derivative_op, precision=lax.Precision.HIGHEST)
    return (filtered.reshape(SCAL_ALL, LG, length), gradient.reshape(SCAL_ALL, LG, length))


def solution(mesh):
    return jax.shard_map(
        on_device,
        mesh=mesh,
        in_specs=(
            P(None, ("table", "scal")),
            P("table", "scal"),
            P(("table", "scal"), None),
            P(("table", "scal")),
        ),
        out_specs=(P(None, ("table", "scal"), None), P(None, ("table", "scal"), None)),
        check_vma=False,
    )
```

profile of v0, /device:TPU:8, one launch (start us, length us, event | category | flops | bytes accessed | tf_op | source)
XLA Modules:
  0.0 340.3 jit_solution(11872699540350610518)
XLA Ops:
  0.6 0.0 copy-start
  0.6 0.5 broadcast.128
  1.2 1.5 reduce.5
  2.6 0.1 reshape_squeeze.3
  2.7 0.1 copy.72
  2.8 1.7 select_reduce_fusion
  4.5 0.1 copy.73
  4.6 0.9 concatenate.9
  5.5 0.7 convert_element_type.26
  6.2 0.1 concatenate.8
  6.3 1.0 fusion.3
  7.3 0.2 copy.75
  7.5 0.1 reshape.102
  7.6 0.3 copy.76
  7.9 0.1 reshape.103
  8.0 0.3 copy.77
  8.3 0.2 reshape.131
  8.5 21.4 %all_to_all.40 = f32[32,1,800]{2,1,0:T(1,128)S(1)} all-to-all(f32[32,1,800]{2,1,0:T(1,128)S(1)} %reshape.131), channel_id=1, replica_groups=mesh['table'=32,'scal'=8] {'table'}, dimensions={0} | all-to-all | bytes 204800 | tf_op jit(solution)/shard_map/all_to_all | solution.py:134
  29.9 0.6 broadcast.129
  30.5 1.0 reduce.6
  31.5 0.1 reshape.132
  31.6 0.1 copy.78
  31.7 0.1 reshape.104
  31.8 14.7 %all_gather.3 = f32[5,40960]{1,0:T(8,128)S(1)} all-gather(f32[5,5120]{1,0:T(8,128)S(1)} %reshape.104), channel_id=1, replica_groups=mesh['table'=32,'scal'=8] {'scal'}, dimensions={1}, use_global_device_ids=true | all-gather | bytes 921600 | tf_op jit(solution)/shard_map/all_gather | solution.py:137
  46.5 0.2 compare_select_fusion
  46.7 2.4 slice_convert_fusion
  49.1 0.0 copy-done
  49.1 134.9 %gather_fusion = f32[40960,128]{1,0:T(8,128)} fusion(f32[4096,128]{1,0:T(8,128)S(1)} %copy-done, s32[40960]{0:T(1024)S(1)} %broadcast_clamp_fusion), kind=kCustom, calls=%fused_computation | custom fusion | bytes 42106880 | tf_op jit(solution)/shard_map/jit(_take)/gather | solution.py:139
  184.1 21.2 %copy.79 = f32[40960,128]{0,1:T(8,128)} copy(f32[40960,128]{1,0:T(8,128)} %gather_fusion) | data formatting | bytes 41943040 | tf_op jit(solution)/shard_map/jit(_take)/gather | solution.py:139
  205.3 0.0 copy-done.4
  205.3 0.0 copy-done.5
  205.3 0.3 pad_maximum_fusion.3
  205.6 0.0 copy-done.3
  205.6 0.6 pad_maximum_fusion.1
  206.2 0.3 broadcast_multiply_fusion.2
  206.5 0.5 broadcast_multiply_fusion.1
  207.0 0.6 pad_maximum_fusion
  207.6 3.4 %broadcast_multiply_fusion = f32[2,2,2,4,40960]{4,3,2,1,0:T(4,128)} fusion(f32[4,40960]{1,0:T(4,128)S(1)} %pad_maximum_fusion, f32[2,2,2,40960]{3,2,1,0:T(2,128)S(1)} %broadcast_multiply_fusion.1), kind=kLoop, calls=%fused_computation.2 | loop fusion | flops 1310720 | bytes 7208960 | tf_op jit(solution)/shard_map/mul | solution.py:31
  211.0 6.1 %mul.131 = f32[32,40960]{1,0:T(8,128)} reshape(f32[2,2,2,4,40960]{4,3,2,1,0:T(4,128)} %broadcast_multiply_fusion) | data formatting | bytes 10485760 | tf_op jit(solution)/shard_map/mul | solution.py:31
  217.2 0.0 copy-done.6
  217.2 0.1 compare_and_fusion
  217.2 10.2 %multiply_reduce_fusion = f32[40960,4]{0,1:T(4,128)S(1)} fusion(f32[40960,4,32]{0,2,1:T(8,128)} %bitcast.56, f32[40960,32]{0,1:T(8,128)} %bitcast.57, pred[40960]{0:T(1024)(128)(4,1)S(1)} %compare_and_fusion), kind=kLoop, calls=%fused_computation.1 | loop fusion | flops 15564800 | bytes 26910720 | tf_op jit(solution)/shard_map/nsk,kn->sn/dot_general | solution.py:141
  227.4 14.6 %all_to_all.41 = f32[4,8,5120]{2,0,1:T(4,128)S(1)} all-to-all(f32[4,8,5120]{2,0,1:T(4,128)S(1)} %bitcast.60), channel_id=1, replica_groups=mesh['table'=32,'scal'=8] {'scal'}, dimensions={1} | all-to-all | bytes 1310720 | tf_op jit(solution)/shard_map/all_to_all | solution.py:143
  242.0 17.7 %reshape.106 = f32[32,32,32,5]{3,2,1,0:T(8,128)} reshape(f32[8,4,1,5120]{3,1,0,2:T(4,128)S(1)} %bitcast.61) | data formatting | bytes 1310720 | tf_op jit(solution)/shard_map/reshape | solution.py:143
  259.7 12.5 %copy.81 = f32[32,32,32,5]{2,0,3,1:T(8,128)} copy(f32[32,32,32,5]{3,2,1,0:T(8,128)} %reshape.106) | data formatting | bytes 1310720 | tf_op jit(solution)/shard_map/reshape | solution.py:143
  272.3 2.7 reshape.133
  275.0 23.3 %all_to_all.42 = f32[32,1,5120]{2,1,0:T(1,128)S(1)} all-to-all(f32[32,1,5120]{2,1,0:T(1,128)S(1)} %reshape.133), channel_id=1, replica_groups=mesh['table'=32,'scal'=8] {'table'}, dimensions={0} | all-to-all | bytes 1310720 | tf_op jit(solution)/shard_map/all_to_all | solution.py:147
  298.3 2.2 reduce.7
  300.5 2.4 reshape.134
  302.9 3.0 copy.82
  305.9 1.5 fusion.2
  307.4 0.4 copy.92
  307.8 0.1 bitcast_bitcast_fusion.1
  307.9 0.5 reshape.135
  308.3 17.0 %all_to_all.43 = f32[32,1,2048]{2,1,0:T(1,128)S(1)} all-to-all(f32[32,1,2048]{2,1,0:T(1,128)S(1)} %reshape.135), channel_id=1, replica_groups=mesh['table'=32,'scal'=8] {'table'}, dimensions={0} | all-to-all | bytes 524288 | tf_op jit(solution)/shard_map/all_to_all | solution.py:152
  325.3 1.3 reduce.8
  326.7 1.3 reshape.136
  328.0 1.4 bitcast_bitcast_fusion
  329.4 0.0 copy-start.7
  329.5 4.3 %copy.85 = f32[32,1,8,32,8]{4,3,2,0,1:T(8,128)} copy(f32[32,1,8,32,8]{0,4,2,3,1:T(8,128)S(1)} %bitcast_bitcast_fusion) | data formatting | bytes 524288 | tf_op jit(solution)/shard_map/all_to_all | solution.py:152
  333.8 4.0 %reshape.109 = f32[256,256]{1,0:T(8,128)S(1)} reshape(f32[32,1,8,32,8]{4,3,2,0,1:T(8,128)} %copy.85) | data formatting | bytes 524288 | tf_op jit(solution)/shard_map/reshape | solution.py:152
  337.8 1.3 fusion.14
  339.2 0.0 copy-start.2
  339.2 1.1 convolution_bitcast_fusion
  (11 shorter events, 0.1 us)
Async XLA Ops:
  0.6 48.5 %copy-start = (f32[4096,128]{1,0:T(8,128)S(1)}, f32[4096,128]{1,0:T(8,128)}, u32[]{:S(2)}) copy-start(f32[4096,128]{1,0:T(8,128)} %param.7) | copy-start | bytes 6291460
  184.1 21.2 %copy-start.4 = (f32[1,40960]{1,0:T(1,128)S(1)}, f32[1,40960]{1,0:T(1,128)}, u32[]{:S(2)}) copy-start(f32[1,40960]{1,0:T(1,128)} %get-tuple-element.5) | copy-start | bytes 491524
  184.1 21.2 %copy-start.5 = (f32[1,40960]{1,0:T(1,128)S(1)}, f32[1,40960]{1,0:T(1,128)}, u32[]{:S(2)}) copy-start(f32[1,40960]{1,0:T(1,128)} %get-tuple-element.10) | copy-start | bytes 491524
  184.1 21.5 %copy-start.3 = (f32[1,40960]{1,0:T(1,128)S(1)}, f32[1,40960]{1,0:T(1,128)}, u32[]{:S(2)}) copy-start(f32[1,40960]{1,0:T(1,128)} %get-tuple-element.12) | copy-start | bytes 491524
  211.0 6.1 %copy-start.6 = (s32[1,40960]{1,0:T(1,128)S(1)}, s32[1,40960]{1,0:T(1,128)}, u32[]{:S(2)}) copy-start(s32[1,40960]{1,0:T(1,128)} %get-tuple-element.2) | copy-start | bytes 491524
  328.0 12.3 %copy-start.1 = (f32[4096,128]{1,0:T(8,128)S(1)}, f32[4096,128]{1,0:T(8,128)}, u32[]{:S(2)}) copy-start(f32[4096,128]{1,0:T(8,128)} %param.7) | copy-start | bytes 6291460
  329.4 9.7 %copy-start.7 = (f32[256,256]{1,0:T(8,128)S(1)}, f32[256,256]{1,0:T(8,128)}, u32[]{:S(2)}) copy-start(f32[256,256]{1,0:T(8,128)} %constant.46.clone) | copy-start | bytes 786436
  339.2 1.1 copy-start.2
where the time goes:
time: 341 us; the launch traced here: 340 us
  local copies, waits for them, and re-layouts  216 us (63%)
  blocking collectives  91.1 us (27%)
  other arithmetic  27 us (8%)
  matrix products  4.91 us (1%)
    gather x2, local copies, waits for them, and re-layouts, on_device(): jnp.take(flamelet_table, shard_piece[0].astype(jnp.int32), axis=0)  156 us
    reshape x2, local copies, waits for them, and re-layouts, on_device(): lax.all_to_all(looked, 'scal', split_axis=1, concat_axis=0, tiled=True)  30.2 us
    all_to_all x1, blocking collectives, on_device(): lax.all_to_all(grouped, 'table', split_axis=1, concat_axis=1, tiled=True)  23.3 us
    all_to_all x1, blocking collectives, on_device(): lax.all_to_all(outgoing, 'table', split_axis=1, concat_axis=1, tiled=True)  21.4 us
    all_to_all x1, blocking collectives, on_device(): lax.all_to_all(values, 'table', split_axis=1, concat_axis=3, tiled=True)  17 us
    all_gather x1, blocking collectives, on_device(): shard_piece = lax.all_gather(received, 'scal', axis=1, tiled=True)  14.7 us
    all_to_all x1, blocking collectives, on_device(): lax.all_to_all(looked, 'scal', split_axis=1, concat_axis=0, tiled=True)  14.6 us
    dot_general x1, other arithmetic, on_device(): jnp.einsum('nsk,kn->sn', table_rows, weights, precision=lax.Precision.HIG...  10.2 us

commit v1 on v0

v1 whole, which is shorter than its diff:
```python
import functools

import jax
import jax.numpy as jnp
import numpy as np
from jax import lax
from jax.experimental import pallas as pl
from jax.experimental.pallas import tpu as pltpu
from jax.sharding import PartitionSpec as P

F32, BF16, I32 = jnp.float32, jnp.bfloat16, jnp.int32
MESH = pl.DeviceIdType.MESH

strength = 0.499


def thomas_solve(below, middle, above, right_side):
    length = middle.shape[0]
    upper_factor = np.zeros(length)
    solved = np.zeros(right_side.shape)
    for row in range(length):
        if row == 0:
            denom = middle[0]
            solved[0] = right_side[0] / denom
        else:
            denom = middle[row] - below[row] * upper_factor[row - 1]
            solved[row] = (right_side[row] - below[row] * solved[row - 1]) / denom
        upper_factor[row] = above[row] / denom
    for row in range(length - 2, -1, -1):
        solved[row] = solved[row] - upper_factor[row] * solved[row + 1]
    return solved


def filter_table(length):
    positions = np.arange(length)
    offset = positions[None, :] - positions[:, None]
    distance = np.abs(offset)
    interior = (positions >= 3) & (positions <= length - 4)
    coeffs = [
        (11.0 + 10.0 * strength) / 16.0,
        (15.0 + 34.0 * strength) / 64.0,
        (-3.0 + 6.0 * strength) / 32.0,
        (1.0 - 2.0 * strength) / 64.0,
    ]
    band = np.zeros((length, length))
    for reach in range(4):
        band = band + np.where(distance == reach, coeffs[reach], 0.0)
    right_side = np.where(interior[:, None], band, np.where(offset == 0, 1.0, 0.0))
    coupling = np.where(interior, strength, 0.0)
    return thomas_solve(coupling, np.ones(length), coupling, right_side)


def derivative_table(length):
    positions = np.arange(length)
    offset = positions[None, :] - positions[:, None]
    distance = np.abs(offset)
    direction = np.sign(offset) * 1.0
    boundary = (positions == 0) | (positions == length - 1)
    second = (positions == 1) | (positions == length - 2)
    interior = ~(boundary | second)
    below_diag = np.where(
        interior, 1.0 / 3.0, np.where(second, 0.25, np.where(positions == length - 1, 2.0, 0.0))
    )
    above_diag = np.where(
        interior, 1.0 / 3.0, np.where(second, 0.25, np.where(positions == 0, 2.0, 0.0))
    )
    inner_rows = direction * (
        np.where(distance == 1, 7.0 / 9.0, 0.0) + np.where(distance == 2, 1.0 / 36.0, 0.0)
    )
    second_rows = direction * np.where(distance == 1, 0.75, 0.0)
    first_row = np.where(
        offset == 0, -2.5, np.where(offset == 1, 2.0, np.where(offset == 2, 0.5, 0.0))
    )
    final_row = np.where(
        offset == 0, 2.5, np.where(offset == -1, -2.0, np.where(offset == -2, -0.5, 0.0))
    )
    right_side = np.where(
        interior[:, None],
        inner_rows,
        np.where(
            second[:, None], second_rows, np.where((positions == 0)[:, None], first_row, final_row)
        ),
    )
    return thomas_solve(below_diag, np.ones(length), above_diag, right_side)


NT = (((1,), (1,)), ((), ()))
TN = (((0,), (0,)), ((), ()))
TABLES = 32
YS = 4
MOST = 5


def split3(x):
    hi = x.astype(BF16).astype(F32)
    rest = x - hi
    mid = rest.astype(BF16).astype(F32)
    return hi, mid, rest - mid


def iota(shape, axis):
    return lax.broadcasted_iota(I32, shape, axis)


def request_kernel(coords_ref, owner_ref, bin_ref, msg_ref, pay_ref, acc5, acc6, acc7):
    pay_ref[0:1, :] = bin_ref[...].astype(F32)
    pay_ref[1:5, :] = coords_ref[...]
    pay_ref[5:8, :] = jnp.zeros((3, pay_ref.shape[1]), F32)
    width = 256
    at, to = iota((width, width), 0), iota((width, width), 1)
    before = jnp.where((at < to) & ((at >> 6) == (to >> 6)), 1.0, 0.0).astype(BF16)
    msg_ref[...] = jnp.zeros_like(msg_ref)
    acc5[...] = jnp.zeros_like(acc5)
    acc6[...] = jnp.zeros_like(acc6)
    acc7[...] = jnp.zeros_like(acc7)

    def chunk(step, carry):
        lanes = pl.ds(pl.multiple_of(step * width, width), width)
        owner = owner_ref[:, lanes]
        pay = pay_ref[:, lanes]
        hit = iota((TABLES, width), 0) == owner
        ones = jnp.where(hit, 1.0, 0.0).astype(BF16)
        ahead = jnp.dot(ones, before, preferred_element_type=F32)
        rank = jnp.sum(jnp.where(hit, ahead, 0.0), axis=0, keepdims=True).astype(I32)
        group = step * (width // 64) + (iota((1, width), 1) >> 6)
        slot = rank * 32 + group
        place = jnp.where(iota((128, width), 0) == slot, 1.0, 0.0).astype(BF16)
        last = jnp.where(hit & (rank == MOST - 1), 1.0, 0.0).astype(BF16)
        mine = iota((TABLES, 8, width), 0) == jnp.broadcast_to(owner[None], (TABLES, 8, width))
        same = (iota((128, width), 0) & 31) == group
        for part in split3(pay):
            left = jnp.where(mine, part[None], 0.0).reshape(TABLES * 8, width).astype(BF16)
            msg_ref[...] += lax.dot_general(left, place, NT, preferred_element_type=F32)
            fields = jnp.concatenate(
                [jnp.broadcast_to(part[f : f + 1], (32, width)) for f in range(4)], axis=0
            )
            right = jnp.where(same, fields, 0.0).astype(BF16)
            acc5[...] += lax.dot_general(last, right, NT, preferred_element_type=F32)
            field = jnp.where(same & (iota((128, width), 0) < 32), part[4:5], 0.0).astype(BF16)
            acc6[...] += lax.dot_general(last, field, NT, preferred_element_type=F32)
        code = (owner * 8 + rank).astype(F32)
        own = jnp.where(iota((TABLES, width), 0) == group, code, 0.0).astype(BF16)
        spot = jnp.where(
            iota((128, width), 0) == (iota((128, width), 1) & 63), 1.0, 0.0
        ).astype(BF16)
        acc7[...] += lax.dot_general(own, spot, NT, preferred_element_type=F32)
        return carry

    lax.fori_loop(0, owner_ref.shape[1] // width, chunk, 0)
    msg_ref[pl.ds(5, TABLES, stride=8), :] = acc5[...]
    msg_ref[pl.ds(6, TABLES, stride=8), :] = acc6[...]
    msg_ref[pl.ds(7, TABLES, stride=8), :] = acc7[...]


def enter(me_t, me_s, with_partner):
    barrier = pltpu.get_barrier_semaphore()

    def greet(step, carry):
        pl.semaphore_signal(
            barrier, inc=1, device_id=(lax.rem(me_t + step, TABLES), me_s), device_id_type=MESH
        )
        return carry

    lax.fori_loop(1, TABLES, greet, 0)
    for step in range(1, YS):
        pl.semaphore_signal(
            barrier, inc=1, device_id=(me_t, lax.rem(me_s + 2 * step, 2 * YS)), device_id_type=MESH
        )
    if with_partner:
        core = lax.rem(me_s, 2)
        pl.semaphore_signal(
            barrier, inc=1, device_id=(me_t, me_s + 1 - 2 * core), device_id_type=MESH
        )
    pl.semaphore_wait(barrier, TABLES - 1 + YS - 1 + (1 if with_partner else 0))


def far_and_near(body):
    def pair(step, carry):
        body(step)
        body(TABLES - step)
        return carry

    lax.fori_loop(1, TABLES // 2, pair, 0)
    body(TABLES // 2)


def exchange_kernel(
    msg_ref, table_ref, got_ref, all_ref, other_ref, local_sem, swap_sem, row_sem, y_send, y_recv
):
    me_t, me_s = lax.axis_index("table"), lax.axis_index("scal")
    core = lax.rem(me_s, 2)
    me_y = lax.div(me_s, 2)
    partner = (me_t, me_s + 1 - 2 * core)
    enter(me_t, me_s, True)
    swap = pltpu.make_async_remote_copy(
        table_ref, other_ref, swap_sem.at[0], swap_sem.at[1], device_id=partner, device_id_type=MESH
    )

    def send(step):
        to = lax.rem(me_t + step, TABLES)
        pltpu.make_async_remote_copy(
            msg_ref.at[to], got_ref.at[me_t], row_sem.at[0], row_sem.at[1],
            device_id=(to, me_s), device_id_type=MESH,
        ).start()

    far_and_near(send)
    own = pltpu.make_async_copy(msg_ref.at[me_t], got_ref.at[me_t], local_sem.at[0])
    own.start()
    swap.start()
    own.wait()
    whole = pltpu.make_async_remote_copy(
        msg_ref.at[pl.ds(0, TABLES - 1)], got_ref.at[pl.ds(0, TABLES - 1)],
        row_sem.at[0], row_sem.at[1], device_id=partner, device_id_type=MESH,
    )
    whole.wait_recv()
    copies = []
    for step in range(1, YS):
        to = lax.rem(me_s + 2 * step, 2 * YS)
        copy = pltpu.make_async_remote_copy(
            got_ref, all_ref.at[me_y], y_send.at[step - 1], y_recv.at[step - 1],
            device_id=(me_t, to), device_id_type=MESH,
        )
        copy.start()
        copies.append(copy)
    keep = pltpu.make_async_copy(got_ref, all_ref.at[me_y], local_sem.at[1])
    keep.start()
    whole.wait_send()
    keep.wait()
    for copy in copies:
        copy.wait()
    swap.wait()


def lookup_kernel(idx_ref, req_ref, near_ref, far_ref, out_ref, near, far, rows0, rows1, acc, pick, sem):
    loads = [
        pltpu.make_async_copy(near_ref, near, sem.at[0]),
        pltpu.make_async_copy(far_ref, far, sem.at[1]),
    ]
    for load in loads:
        load.start()
    core = lax.rem(lax.axis_index("scal"), 2)
    slots = 32 * MOST
    k, lane = iota((256, 128), 0), iota((256, 128), 1)
    half = jnp.where((k >> 7) == 0, core, 1 - core)
    base = half * 4 + ((k >> 5) & 3)
    for b in range(16):
        pick[b] = jnp.where(lane == base + 8 * b, 1.0, 0.0).astype(BF16)
    for load in loads:
        load.wait()
    spread = jnp.where((iota((96, 128), 0) & 31) == (iota((96, 128), 1) & 31), 1.0, 0.0).astype(BF16)
    kk = iota((32, 256), 0)

    def block(b, base_block):
        blk = base_block + b
        for i in range(slots):
            row = idx_ref[2 * blk + (i // 128), i % 128]
            rows0[i : i + 1, :] = near[pl.ds(row, 1), :]
            rows1[i : i + 1, :] = far[pl.ds(row, 1), :]
        tile = req_ref[blk]
        tail = tile[5:6]
        f = [
            jnp.concatenate([tile[1 + n : 2 + n], extra], axis=1)
            for n, extra in enumerate(
                (pltpu.roll(tail, 96, 1), pltpu.roll(tail, 64, 1), pltpu.roll(tail, 32, 1), tile[6:7])
            )
        ]
        lin = [
            jnp.where(((kk >> bit) & 1) == 0, 1.0 - f[n], f[n]) for n, bit in enumerate((4, 3, 2))
        ]
        last = f[3]
        square = last * last
        cube = square * last
        remain = 1.0 - last
        cubic = (
            remain * remain * remain * (1.0 / 6.0),
            (3.0 * cube - 6.0 * square + 4.0) * (1.0 / 6.0),
            (-3.0 * cube + 3.0 * square + 3.0 * last + 1.0) * (1.0 / 6.0),
            cube * (1.0 / 6.0),
        )
        d = kk & 3
        bent = jnp.where(
            d < 2, jnp.where(d == 0, cubic[0], cubic[1]), jnp.where(d == 2, cubic[2], cubic[3])
        )
        weight = lin[0] * lin[1] * lin[2] * bent
        parts = jnp.concatenate([part.astype(BF16) for part in split3(weight)], axis=0)
        wide = lax.dot_general(parts[:, :slots], spread, TN, preferred_element_type=F32)
        left, right = rows0[...] * wide, rows1[...] * wide
        left_hi, right_hi = left.astype(BF16), right.astype(BF16)
        left_lo = (left - left_hi.astype(F32)).astype(BF16)
        right_lo = (right - right_hi.astype(F32)).astype(BF16)
        chosen = pick[b]
        acc[...] += jnp.dot(
            jnp.concatenate([left_hi, right_hi], axis=1), chosen, preferred_element_type=F32
        ) + jnp.dot(jnp.concatenate([left_lo, right_lo], axis=1), chosen, preferred_element_type=F32)
        return base_block

    def section(step, carry):
        acc[...] = jnp.zeros_like(acc)
        lax.fori_loop(0, 16, block, step * 16)
        y, half_t = step // 2, lax.rem(step, 2)
        for q in range(MOST):
            for g in range(32):
                out_ref[y, g, half_t, q : q + 1, :] = acc[q * 32 + g : q * 32 + g + 1, :]
        return carry

    lax.fori_loop(0, 2 * YS, section, 0)


def reply_kernel(out_ref, got_ref, mid_ref, y_send, y_recv, row_sem, local_sem):
    me_t, me_s = lax.axis_index("table"), lax.axis_index("scal")
    me_y = lax.div(me_s, 2)
    enter(me_t, me_s, False)
    copies = []
    for step in range(1, YS):
        to_y = lax.rem(me_y + step, YS)
        copy = pltpu.make_async_remote_copy(
            out_ref.at[to_y], mid_ref.at[me_y], y_send.at[step - 1], y_recv.at[step - 1],
            device_id=(me_t, lax.rem(me_s + 2 * step, 2 * YS)), device_id_type=MESH,
        )
        copy.start()
        copies.append(copy)

    def pass_on(source, y):
        def send(step):
            to = lax.rem(me_t + step, TABLES)
            pltpu.make_async_remote_copy(
                source.at[to], got_ref.at[me_t, y], row_sem.at[0], row_sem.at[1],
                device_id=(to, me_s), device_id_type=MESH,
            ).start()

        far_and_near(send)

    keeps = [pltpu.make_async_copy(out_ref.at[me_y, me_t], got_ref.at[me_t, me_y], local_sem.at[0])]
    keeps[0].start()
    pass_on(out_ref.at[me_y], me_y)
    for step in range(1, YS):
        copies[step - 1].wait_recv()
        y = lax.rem(me_y + YS - step, YS)
        pass_on(mid_ref.at[y], y)
        keep = pltpu.make_async_copy(mid_ref.at[y, me_t], got_ref.at[me_t, y], local_sem.at[step])
        keep.start()
        keeps.append(keep)
    for keep in keeps:
        keep.wait()
    for copy in copies:
        copy.wait_send()
    whole = pltpu.make_async_remote_copy(
        got_ref.at[pl.ds(0, TABLES - 1)], got_ref.at[pl.ds(0, TABLES - 1)],
        row_sem.at[0], row_sem.at[1],
        device_id=(me_t, lax.rem(me_s + 2, 2 * YS)), device_id_type=MESH,
    )
    whole.wait_send()
    whole.wait_recv()


def filter_kernel(got_ref, code_ref, ops_ref, fil_ref, grad_ref, flat, turned, pencil):
    for y in range(YS):
        for half_t in range(2):
            at = 2 * y + half_t
            for o in range(TABLES):
                flat[at, o * 8 : o * 8 + MOST, :] = got_ref[o, y, half_t]
            turned[at] = flat[at].T

    lane = iota((8, 128), 1)

    def line_block(half_t):
        for y in range(YS):
            at = 2 * y + half_t
            sums = [jnp.zeros((8, 128), F32) for _ in range(8)]
            for b in range(16):
                code = code_ref[half_t * 16 + b, 7:8, :].astype(I32)
                code = jnp.broadcast_to(code, (8, 128))
                low = code & 127
                near = jnp.take_along_axis(turned[at, b * 8 : b * 8 + 8, 0:128], low, axis=1)
                far = jnp.take_along_axis(turned[at, b * 8 : b * 8 + 8, 128:256], low, axis=1)
                cells = jnp.where(code < 128, near, far)
                for r in range(8):
                    moved = pltpu.roll(cells, ((b - r) * 8) % 128, 1)
                    sums[r] = jnp.where((lane >> 3) == b, moved, sums[r])
            for r in range(8):
                pencil[half_t, pl.ds(y * 64 + r, 8, stride=8), :] = sums[r]

    line_block(0)
    line_block(1)
    values = jnp.concatenate([pencil[0], pencil[1]], axis=1)
    fil_ref[...] = jnp.dot(
        values, ops_ref[:, 0:256], precision=lax.Precision.HIGHEST, preferred_element_type=F32
    )
    grad_ref[...] = jnp.dot(
        values, ops_ref[:, 256:512], precision=lax.Precision.HIGHEST, preferred_element_type=F32
    )


def on_device(cell_coords, flamelet_table, owner_shard, local_bin):
    cells = cell_coords.shape[1]
    bins = flamelet_table.shape[0]
    dma = pltpu.SemaphoreType.DMA
    vmem = pl.BlockSpec(memory_space=pltpu.VMEM)
    anywhere = pl.BlockSpec(memory_space=pl.ANY)
    shape = jax.ShapeDtypeStruct
    msg = pl.pallas_call(
        request_kernel,
        out_shape=shape((TABLES * 8, 128), F32),
        in_specs=[vmem] * 3,
        out_specs=vmem,
        scratch_shapes=[
            pltpu.VMEM((8, cells), F32),
            pltpu.VMEM((TABLES, 128), F32),
            pltpu.VMEM((TABLES, 128), F32),
            pltpu.VMEM((TABLES, 128), F32),
        ],
        name="build_requests",
    )(cell_coords, owner_shard.T, local_bin.reshape(1, cells))
    got, everything, other = pl.pallas_call(
        exchange_kernel,
        out_shape=(
            shape((TABLES, 8, 128), F32),
            shape((YS, TABLES, 8, 128), F32),
            shape((bins, 128), F32),
        ),
        in_specs=[anywhere] * 2,
        out_specs=(anywhere,) * 3,
        scratch_shapes=[dma((2,)), dma((2,)), dma((2,)), dma((YS - 1,)), dma((YS - 1,))],
        compiler_params=pltpu.CompilerParams(collective_id=0, has_side_effects=True),
        name="exchange_requests",
    )(msg.reshape(TABLES, 8, 128), flamelet_table)
    rows = everything.reshape(YS * TABLES, 8, 128)
    index = jnp.stack([rows[:, 0], rows[:, 5]], axis=1).astype(I32).reshape(2 * YS * TABLES, 128)
    out = pl.pallas_call(
        lookup_kernel,
        out_shape=shape((YS, TABLES, 2, MOST, 128), F32),
        in_specs=[pl.BlockSpec(memory_space=pltpu.SMEM), vmem, anywhere, anywhere],
        out_specs=vmem,
        scratch_shapes=[
            pltpu.VMEM((bins, 128), F32),
            pltpu.VMEM((bins, 128), F32),
            pltpu.VMEM((32 * MOST, 128), F32),
            pltpu.VMEM((32 * MOST, 128), F32),
            pltpu.VMEM((32 * MOST, 128), F32),
            pltpu.VMEM((16, 256, 128), BF16),
            dma((2,)),
        ],
        name="look_up",
    )(index, rows, flamelet_table, other)
    back, _ = pl.pallas_call(
        reply_kernel,
        out_shape=(
            shape((TABLES, YS, 2, MOST, 128), F32),
            shape((YS, TABLES, 2, MOST, 128), F32),
        ),
        in_specs=[anywhere],
        out_specs=(anywhere,) * 2,
        scratch_shapes=[dma((YS - 1,)), dma((YS - 1,)), dma((2,)), dma((YS,))],
        compiler_params=pltpu.CompilerParams(collective_id=1, has_side_effects=True),
        name="send_replies",
    )(out)
    length = 8 * TABLES
    filter_op = filter_table(length)
    ops = np.concatenate([filter_op.T, (derivative_table(length) @ filter_op).T], axis=1)
    filtered, gradient = pl.pallas_call(
        filter_kernel,
        out_shape=(shape((256, length), F32), shape((256, length), F32)),
        in_specs=[vmem] * 3,
        out_specs=(vmem,) * 2,
        scratch_shapes=[
            pltpu.VMEM((2 * YS, 256, 128), F32),
            pltpu.VMEM((2 * YS, 128, 256), F32),
            pltpu.VMEM((2, 256, 128), F32),
        ],
        name="place_and_filter",
    )(back, got, jnp.asarray(ops.astype(np.float32)))
    return filtered.reshape(32, 8, length), gradient.reshape(32, 8, length)


def solution(mesh):
    return jax.shard_map(
        on_device,
        mesh=mesh,
        in_specs=(
            P(None, ("table", "scal")),
            P("table", "scal"),
            P(("table", "scal"), None),
            P(("table", "scal")),
        ),
        out_specs=(P(None, ("table", "scal"), None), P(None, ("table", "scal"), None)),
        check_vma=False,
    )
```

time: 341 us -> 131 us (0.38)
  local copies, waits for them, and re-layouts: 216 us -> 1.29 us
  Pallas kernels: 0 us -> 127 us
  blocking collectives: 91.1 us -> 0 us
  other arithmetic: 27 us -> 0.78 us
  matrix products: 4.91 us -> 0 us
    gather x2 -> x0, local copies, waits for them, and re-layouts: 156 us -> none  [on_device(): jnp.take(flamelet_table, shard_piece[0].astype(jnp.int32), axis=0)]
    pallas_call x0 -> x5, Pallas kernels: none -> 127 us  [the longest x1 65.6 us: on_device(): pl.pallas_call(lookup_kernel, out_shape=shape((YS, TABLES, 2, MOST, 128),...]
    all_to_all x4 -> x0, blocking collectives: 76.4 us -> none  [the longest x1 23.3 us: on_device(): lax.all_to_all(grouped, 'table', split_axis=1, concat_axis=1, tiled=True)]
    reshape x9 -> x0, local copies, waits for them, and re-layouts: 38.2 us -> none  [the longest x2 30.2 us: on_device(): lax.all_to_all(looked, 'scal', split_axis=1, concat_axis=0, tiled=True)]
    all_gather x1 -> x0, blocking collectives: 14.7 us -> none  [on_device(): shard_piece = lax.all_gather(received, 'scal', axis=1, tiled=True)]
    dot_general x1 -> x0, other arithmetic: 10.2 us -> none  [on_device(): jnp.einsum('nsk,kn->sn', table_rows, weights, precision=lax.Precision.HIG...]
    unnamed x24 -> x0, local copies, waits for them, and re-layouts: 7.82 us -> none
    all_to_all x4 -> x0, local copies, waits for them, and re-layouts: 6.44 us -> none  [the longest x2 5.79 us: on_device(): lax.all_to_all(values, 'table', split_axis=1, concat_axis=3, tiled=True)]
where the time goes in v1:
time: 131 us; the launch traced here: 130 us
  Pallas kernels  127 us (97%)
    pallas_call x1, Pallas kernels, on_device(): pl.pallas_call(lookup_kernel, out_shape=shape((YS, TABLES, 2, MOST, 128),...  65.6 us
    pallas_call x1, Pallas kernels, on_device(): pl.pallas_call(reply_kernel, out_shape=(shape((TABLES, YS, 2, MOST, 128),...  23.1 us
    pallas_call x1, Pallas kernels, on_device(): pl.pallas_call(exchange_kernel, out_shape=(shape((TABLES, 8, 128), F32),...  23 us
    pallas_call x1, Pallas kernels, on_device(): pl.pallas_call(filter_kernel, out_shape=(shape((256, length), F32), shape...  9.95 us
    pallas_call x1, Pallas kernels, on_device(): pl.pallas_call(request_kernel, out_shape=shape((TABLES * 8, 128), F32), i...  5.6 us

profile of v1, /device:TPU:8, one launch (start us, length us, event | category | flops | bytes accessed | tf_op | source)
XLA Modules:
  0.0 130.0 jit_solution(9502453383049627237)
XLA Ops:
  0.6 5.6 %build_requests.1 = f32[256,128]{1,0:T(8,128)} custom-call(f32[4,2048]{1,0:T(4,128)} %coords_ref.1, s32[1,2048]{1,0:T(1,128)} %bitcast.11, s32[1,2048]{1,0:T(1,128)} %bitcast.12), custom_call_target="tpu_custom_call" | custom-call | tf_op jit(solution)/shard_map/build_requests/pallas_call | solution.py:401
  6.2 23.0 %exchange_requests.1 = (f32[32,8,128]{2,1,0:T(8,128)}, f32[4,32,8,128]{3,2,1,0:T(8,128)}, f32[4096,128]{1,0:T(8,128)}) custom-call(f32[32,8,128]{2,1,0:T(8,128)} %bitcast.10, f32[4096,128]{1,0:T(8,128)} %near_ref.1), custom_call_target="tpu_custom_call" | custom-call | tf_op jit(solution)/shard_map/exchange_requests/pallas_call | solution.py:414
  29.3 1.3 fusion
  30.6 0.8 maximum_convert_fusion
  31.3 65.6 %look_up.1.out_ref = f32[4,32,2,5,128]{4,3,2,1,0:T(8,128)} custom-call(s32[256,128]{1,0:T(8,128)} %bitcast.9, f32[128,8,128]{2,1,0:T(8,128)} %bitcast.8, f32[4096,128]{1,0:T(8,128)} %near_ref.1, f32[4096,128]{1,0:T(8,128)} %get-tuple-element.9.far_ref), custom_call_target="tpu_custom_call" | custom-call | tf_op jit(solution)/shard_map/look_up/pallas_call | solution.py:429
  96.9 23.1 %send_replies.1 = (f32[32,4,2,5,128]{4,3,2,1,0:T(8,128)}, f32[4,32,2,5,128]{4,3,2,1,0:T(8,128)}) custom-call(f32[4,32,2,5,128]{4,3,2,1,0:T(8,128)} %look_up.1.out_ref), custom_call_target="tpu_custom_call" | custom-call | tf_op jit(solution)/shard_map/send_replies/pallas_call | solution.py:445
  120.0 9.9 %place_and_filter.1 = (f32[256,256]{1,0:T(8,128)}, f32[256,256]{1,0:T(8,128)}) custom-call(f32[32,4,2,5,128]{4,3,2,1,0:T(8,128)} %get-tuple-element.10.got_ref, f32[32,8,128]{2,1,0:T(8,128)} %get-tuple-element.11.code_ref, f32[256,512]{1,0:T(8,128)} %constant.2.clone.ops_ref), custom_call_target="tpu_custom_call" | custom-call | tf_op jit(solution)/shard_map/place_and_filter/pallas_call | solution.py:460

commit v2 on v1

--- a/solution.py
+++ b/solution.py
@@ -141,7 +141,7 @@
         code = (owner * 8 + rank).astype(F32)
         own = jnp.where(iota((TABLES, width), 0) == group, code, 0.0).astype(BF16)
         spot = jnp.where(
-            iota((128, width), 0) == (iota((128, width), 1) & 63), 1.0, 0.0
+            (iota((128, width), 0) & 63) == (iota((128, width), 1) & 63), 1.0, 0.0
         ).astype(BF16)
         acc7[...] += lax.dot_general(own, spot, NT, preferred_element_type=F32)
         return carry
@@ -231,7 +231,38 @@
     swap.wait()
 
 
-def lookup_kernel(idx_ref, req_ref, near_ref, far_ref, out_ref, near, far, rows0, rows1, acc, pick, sem):
+def slot_weights(tile, spread):
+    tail = tile[5:6]
+    f = [
+        jnp.concatenate([tile[1 + n : 2 + n], extra], axis=1)
+        for n, extra in enumerate(
+            (pltpu.roll(tail, 96, 1), pltpu.roll(tail, 64, 1), pltpu.roll(tail, 32, 1), tile[6:7])
+        )
+    ]
+    last = f[3]
+    square = last * last
+    cube = square * last
+    remain = 1.0 - last
+    cubic = (
+        remain * remain * remain * (1.0 / 6.0),
+        (3.0 * cube - 6.0 * square + 4.0) * (1.0 / 6.0),
+        (-3.0 * cube + 3.0 * square + 3.0 * last + 1.0) * (1.0 / 6.0),
+        cube * (1.0 / 6.0),
+    )
+    sub = iota((8, 256), 0)
+    d = sub & 3
+    inner = jnp.where(
+        d < 2, jnp.where(d == 0, cubic[0], cubic[1]), jnp.where(d == 2, cubic[2], cubic[3])
+    ) * jnp.where(sub < 4, 1.0 - f[2], f[2])
+    first, second = (1.0 - f[0], f[0]), (1.0 - f[1], f[1])
+    weight = jnp.concatenate([(one * two) * inner for one in first for two in second], axis=0)
+    high = weight.astype(BF16)
+    parts = jnp.concatenate([high, (weight - high.astype(F32)).astype(BF16)], axis=0)
+    return lax.dot_general(parts[:, : 32 * MOST], spread, TN, preferred_element_type=F32)
+
+
+def lookup_kernel(idx_ref, req_ref, near_ref, far_ref, out_ref, near, far, table, rows, wide, acc, pick, sem):
+    bins = near_ref.shape[0]
     loads = [
         pltpu.make_async_copy(near_ref, near, sem.at[0]),
         pltpu.make_async_copy(far_ref, far, sem.at[1]),
@@ -242,67 +273,72 @@
     slots = 32 * MOST
     k, lane = iota((256, 128), 0), iota((256, 128), 1)
     half = jnp.where((k >> 7) == 0, core, 1 - core)
-    base = half * 4 + ((k >> 5) & 3)
-    for b in range(16):
-        pick[b] = jnp.where(lane == base + 8 * b, 1.0, 0.0).astype(BF16)
+    shifted = lane - (half * 4 + ((k >> 5) & 3))
+
+    def choose(b, carry):
+        pick[b] = jnp.where(shifted == 8 * b, 1.0, 0.0).astype(BF16)
+        return carry
+
+    lax.fori_loop(0, 16, choose, 0)
     for load in loads:
         load.wait()
-    spread = jnp.where((iota((96, 128), 0) & 31) == (iota((96, 128), 1) & 31), 1.0, 0.0).astype(BF16)
-    kk = iota((32, 256), 0)
-
-    def block(b, base_block):
-        blk = base_block + b
-        for i in range(slots):
-            row = idx_ref[2 * blk + (i // 128), i % 128]
-            rows0[i : i + 1, :] = near[pl.ds(row, 1), :]
-            rows1[i : i + 1, :] = far[pl.ds(row, 1), :]
-        tile = req_ref[blk]
-        tail = tile[5:6]
-        f = [
-            jnp.concatenate([tile[1 + n : 2 + n], extra], axis=1)
-            for n, extra in enumerate(
-                (pltpu.roll(tail, 96, 1), pltpu.roll(tail, 64, 1), pltpu.roll(tail, 32, 1), tile[6:7])
-            )
-        ]
-        lin = [
-            jnp.where(((kk >> bit) & 1) == 0, 1.0 - f[n], f[n]) for n, bit in enumerate((4, 3, 2))
-        ]
-        last = f[3]
-        square = last * last
-        cube = square * last
-        remain = 1.0 - last
-        cubic = (
-            remain * remain * remain * (1.0 / 6.0),
-            (3.0 * cube - 6.0 * square + 4.0) * (1.0 / 6.0),
-            (-3.0 * cube + 3.0 * square + 3.0 * last + 1.0) * (1.0 / 6.0),
-            cube * (1.0 / 6.0),
-        )
-        d = kk & 3
-        bent = jnp.where(
-            d < 2, jnp.where(d == 0, cubic[0], cubic[1]), jnp.where(d == 2, cubic[2], cubic[3])
-        )
-        weight = lin[0] * lin[1] * lin[2] * bent
-        parts = jnp.concatenate([part.astype(BF16) for part in split3(weight)], axis=0)
-        wide = lax.dot_general(parts[:, :slots], spread, TN, preferred_element_type=F32)
-        left, right = rows0[...] * wide, rows1[...] * wide
+
+    def weave(step, carry):
+        for part in range(8):
+            at = pl.multiple_of(step * 64 + part * 8, 8)
+            table[pl.ds(2 * at + 8, 8, stride=2), :] = near[pl.ds(at, 8), :]
+            table[pl.ds(2 * at + 9, 8, stride=2), :] = far[pl.ds(at, 8), :]
+        return carry
+
+    lax.fori_loop(0, bins // 64, weave, 0)
+    spread = jnp.where((iota((64, 128), 0) & 31) == (iota((64, 128), 1) & 31), 1.0, 0.0).astype(BF16)
+
+    pair_of = iota((8, 128), 0) >> 1
+
+    def fetch(blk, slot):
+        for at in range(0, slots, 4):
+            group = None
+            for r in range(4):
+                row = idx_ref[2 * blk + ((at + r) // 128), (at + r) % 128]
+                piece = table[pl.ds(row + (8 - 2 * r), 8), :]
+                group = piece if r == 0 else jnp.where(pair_of == r, piece, group)
+            rows[slot, 2 * at : 2 * at + 8, :] = group
+        wide[slot] = slot_weights(req_ref[blk], spread)
+
+    def contract(b, slot):
+        left = rows[slot, pl.ds(0, slots, stride=2), :] * wide[slot]
+        right = rows[slot, pl.ds(1, slots, stride=2), :] * wide[slot]
         left_hi, right_hi = left.astype(BF16), right.astype(BF16)
         left_lo = (left - left_hi.astype(F32)).astype(BF16)
         right_lo = (right - right_hi.astype(F32)).astype(BF16)
         chosen = pick[b]
-        acc[...] += jnp.dot(
+        return jnp.dot(
             jnp.concatenate([left_hi, right_hi], axis=1), chosen, preferred_element_type=F32
         ) + jnp.dot(jnp.concatenate([left_lo, right_lo], axis=1), chosen, preferred_element_type=F32)
-        return base_block
 
     def section(step, carry):
         acc[...] = jnp.zeros_like(acc)
-        lax.fori_loop(0, 16, block, step * 16)
+
+        def four(j, base):
+            b = 4 * j
+            blk = base + b
+            fetch(blk + 2, 2)
+            fetch(blk + 3, 3)
+            acc[...] += contract(b, 0) + contract(b + 1, 1)
+            fetch(jnp.minimum(blk + 4, 2 * YS * 16 - 1), 0)
+            fetch(jnp.minimum(blk + 5, 2 * YS * 16 - 1), 1)
+            acc[...] += contract(b + 2, 2) + contract(b + 3, 3)
+            return base
+
+        lax.fori_loop(0, 4, four, step * 16)
         y, half_t = step // 2, lax.rem(step, 2)
         for q in range(MOST):
             for g in range(32):
                 out_ref[y, g, half_t, q : q + 1, :] = acc[q * 32 + g : q * 32 + g + 1, :]
         return carry
 
+    fetch(0, 0)
+    fetch(1, 1)
     lax.fori_loop(0, 2 * YS, section, 0)
 
 
@@ -363,25 +399,32 @@
 
     lane = iota((8, 128), 1)
 
-    def line_block(half_t):
+    def cells_of(at, t, b):
+        code = jnp.broadcast_to(code_ref[t, 7:8, :].astype(I32), (8, 128))
+        low = code & 127
+        near = jnp.take_along_axis(turned[at, b * 8 : b * 8 + 8, 0:128], low, axis=1)
+        far = jnp.take_along_axis(turned[at, b * 8 : b * 8 + 8, 128:256], low, axis=1)
+        return jnp.where(code < 128, near, far)
+
+    for half_t in range(2):
         for y in range(YS):
             at = 2 * y + half_t
-            sums = [jnp.zeros((8, 128), F32) for _ in range(8)]
-            for b in range(16):
-                code = code_ref[half_t * 16 + b, 7:8, :].astype(I32)
-                code = jnp.broadcast_to(code, (8, 128))
-                low = code & 127
-                near = jnp.take_along_axis(turned[at, b * 8 : b * 8 + 8, 0:128], low, axis=1)
-                far = jnp.take_along_axis(turned[at, b * 8 : b * 8 + 8, 128:256], low, axis=1)
-                cells = jnp.where(code < 128, near, far)
-                for r in range(8):
-                    moved = pltpu.roll(cells, ((b - r) * 8) % 128, 1)
-                    sums[r] = jnp.where((lane >> 3) == b, moved, sums[r])
+            tiles = [
+                jnp.where(
+                    lane < 64, cells_of(at, half_t * 16 + b, b), cells_of(at, half_t * 16 + b + 8, b + 8)
+                )
+                for b in range(8)
+            ]
+            for bit in (1, 2, 4):
+                keep = ((lane >> 3) & bit) == 0
+                for i in range(8):
+                    if not i & bit:
+                        one, two = tiles[i], tiles[i + bit]
+                        tiles[i] = jnp.where(keep, one, pltpu.roll(two, 8 * bit, 1))
+                        tiles[i + bit] = jnp.where(keep, pltpu.roll(one, 128 - 8 * bit, 1), two)
             for r in range(8):
-                pencil[half_t, pl.ds(y * 64 + r, 8, stride=8), :] = sums[r]
-
-    line_block(0)
-    line_block(1)
+                pencil[half_t, pl.ds(y * 64 + r, 8, stride=8), :] = tiles[r]
+
     values = jnp.concatenate([pencil[0], pencil[1]], axis=1)
     fil_ref[...] = jnp.dot(
         values, ops_ref[:, 0:256], precision=lax.Precision.HIGHEST, preferred_element_type=F32
@@ -425,7 +468,7 @@
         name="exchange_requests",
     )(msg.reshape(TABLES, 8, 128), flamelet_table)
     rows = everything.reshape(YS * TABLES, 8, 128)
-    index = jnp.stack([rows[:, 0], rows[:, 5]], axis=1).astype(I32).reshape(2 * YS * TABLES, 128)
+    index = jnp.stack([rows[:, 0], rows[:, 5]], axis=1).astype(I32).reshape(2 * YS * TABLES, 128) * 2
     out = pl.pallas_call(
         lookup_kernel,
         out_shape=shape((YS, TABLES, 2, MOST, 128), F32),
@@ -434,8 +477,9 @@
         scratch_shapes=[
             pltpu.VMEM((bins, 128), F32),
             pltpu.VMEM((bins, 128), F32),
-            pltpu.VMEM((32 * MOST, 128), F32),
-            pltpu.VMEM((32 * MOST, 128), F32),
+            pltpu.VMEM((2 * bins + 16, 128), F32),
+            pltpu.VMEM((4, 2 * 32 * MOST, 128), F32),
+            pltpu.VMEM((4, 32 * MOST, 128), F32),
             pltpu.VMEM((32 * MOST, 128), F32),
             pltpu.VMEM((16, 256, 128), BF16),
             dma((2,)),

time: 131 us -> 94.1 us (0.72)
  Pallas kernels: 127 us -> 90 us
    pallas_call x1, Pallas kernels: 65.6 us -> 34.3 us  [on_device(): pl.pallas_call(lookup_kernel, out_shape=shape((YS, TABLES, 2, MOST, 128),...]
    pallas_call x1, Pallas kernels: 9.95 us -> 4.07 us  [on_device(): pl.pallas_call(filter_kernel, out_shape=(shape((256, length), F32), shape...]
where the time goes in v2:
time: 94.1 us; the launch traced here: 92.7 us
  Pallas kernels  90 us (96%)
  local copies, waits for them, and re-layouts  1.29 us (1%)
    pallas_call x1, Pallas kernels, on_device(): pl.pallas_call(lookup_kernel, out_shape=shape((YS, TABLES, 2, MOST, 128),...  34.3 us
    pallas_call x1, Pallas kernels, on_device(): pl.pallas_call(exchange_kernel, out_shape=(shape((TABLES, 8, 128), F32),...  23 us
    pallas_call x1, Pallas kernels, on_device(): pl.pallas_call(reply_kernel, out_shape=(shape((TABLES, YS, 2, MOST, 128),...  22.9 us
    pallas_call x1, Pallas kernels, on_device(): pl.pallas_call(request_kernel, out_shape=shape((TABLES * 8, 128), F32), i...  5.73 us
    pallas_call x1, Pallas kernels, on_device(): pl.pallas_call(filter_kernel, out_shape=(shape((256, length), F32), shape...  4.07 us

profile of v2, /device:TPU:8, one launch (start us, length us, event | category | flops | bytes accessed | tf_op | source)
XLA Modules:
  0.0 92.7 jit_solution(8788240660938307558)
XLA Ops:
  0.6 5.7 %build_requests.1 = f32[256,128]{1,0:T(8,128)} custom-call(f32[4,2048]{1,0:T(4,128)} %coords_ref.1, s32[1,2048]{1,0:T(1,128)} %bitcast.11, s32[1,2048]{1,0:T(1,128)} %bitcast.12), custom_call_target="tpu_custom_call" | custom-call | tf_op jit(solution)/shard_map/build_requests/pallas_call | solution.py:444
  6.4 23.0 %exchange_requests.1 = (f32[32,8,128]{2,1,0:T(8,128)}, f32[4,32,8,128]{3,2,1,0:T(8,128)}, f32[4096,128]{1,0:T(8,128)}) custom-call(f32[32,8,128]{2,1,0:T(8,128)} %bitcast.10, f32[4096,128]{1,0:T(8,128)} %near_ref.1), custom_call_target="tpu_custom_call" | custom-call | tf_op jit(solution)/shard_map/exchange_requests/pallas_call | solution.py:457
  29.4 1.3 %fusion.1 = (f32[128,1,128]{2,1,0:T(1,128)S(1)}, f32[128,1,128]{2,1,0:T(1,128)S(1)}) fusion(f32[128,8,128]{2,1,0:T(8,128)} %bitcast.7), kind=kLoop, calls=%fused_computation.2 | loop fusion | bytes 262144 | tf_op jit(solution)/shard_map/slice | solution.py:471
  30.7 0.8 fusion
  31.5 34.3 %look_up.1.out_ref = f32[4,32,2,5,128]{4,3,2,1,0:T(8,128)} custom-call(s32[256,128]{1,0:T(8,128)} %bitcast.9, f32[128,8,128]{2,1,0:T(8,128)} %bitcast.8, f32[4096,128]{1,0:T(8,128)} %near_ref.1, f32[4096,128]{1,0:T(8,128)} %get-tuple-element.9.far_ref), custom_call_target="tpu_custom_call" | custom-call | tf_op jit(solution)/shard_map/look_up/pallas_call | solution.py:472
  65.8 22.9 %send_replies.1 = (f32[32,4,2,5,128]{4,3,2,1,0:T(8,128)}, f32[4,32,2,5,128]{4,3,2,1,0:T(8,128)}) custom-call(f32[4,32,2,5,128]{4,3,2,1,0:T(8,128)} %look_up.1.out_ref), custom_call_target="tpu_custom_call" | custom-call | tf_op jit(solution)/shard_map/send_replies/pallas_call | solution.py:489
  88.6 4.1 %place_and_filter.1 = (f32[256,256]{1,0:T(8,128)}, f32[256,256]{1,0:T(8,128)}) custom-call(f32[32,4,2,5,128]{4,3,2,1,0:T(8,128)} %get-tuple-element.10.got_ref, f32[32,8,128]{2,1,0:T(8,128)} %get-tuple-element.11.code_ref, f32[256,512]{1,0:T(8,128)} %constant.4.clone.ops_ref), custom_call_target="tpu_custom_call" | custom-call | tf_op jit(solution)/shard_map/place_and_filter/pallas_call | solution.py:504
